TPU v7x, 32 devices: a whole 2x2x4 slice. The times are simulated.
32 devices in a mesh: groups: 2 (over x), long: 16 (over z, y, core).
Axes of the slice: x: 2, y: 2, z: 4, core: 2. Of those that a mesh axis runs over, the one named last changes fastest.
Arguments:
- initial_state: float32 [2, 8192, 128], P(None, ('groups', 'long')), parts along dimension 1, may hold values from -6 to 6
- adjoint_state: float32 [2, 8192, 128], P(None, ('groups', 'long')), parts along dimension 1, may hold values from -6 to 6
- current_gates: float32 [8, 2, 128, 128], P('groups'), parts along dimension 0, may hold values from -0.375 to 0.375
Outputs:
- final_state: float32 [2, 8192, 128], P(None, ('groups', 'long')), parts along dimension 1
- final_adjoint: float32 [2, 8192, 128], P(None, ('groups', 'long')), parts along dimension 1
There are 2 independent parts, one for each index of `groups`. A program takes and returns all parts, laid end to end along the dimension named above; each array names one. Nothing has to cross between parts.
All inputs are finite; a program needn't handle non-finite values.
Results may differ from a plain program's by a relative error of at most 0.00017.
Values sent between devices are 32-bit elements; how exact they have to be, the bound alone decides.
A program may use at most 64 MiB of HBM per device.

v0:
```python
import functools

import jax
import jax.numpy as jnp
from jax import lax
from jax.experimental import pallas as pl
from jax.experimental.pallas import tpu as pltpu
from jax.sharding import PartitionSpec as P

SECTIONS = 4
NS_ITERS = 8
MESH = pl.DeviceIdType.MESH
ADJ_IN, PSI_IN, RS, AG, MID, ADJ_OUT, PSI_OUT = 0, 1, 2, 6, 10, 14, 15


def split(x):
    high = x.astype(jnp.bfloat16)
    return high, (x - high.astype(jnp.float32)).astype(jnp.bfloat16)


def dot3(left, right, contract):
    def dot(a, b):
        return lax.dot_general(
            a, b, (contract, ((), ())), preferred_element_type=jnp.float32
        )

    return dot(left[0], right[0]) + (dot(left[0], right[1]) + dot(left[1], right[0]))


def embed_out(real, imag):
    return jnp.concatenate(
        [
            jnp.concatenate([real, -imag], axis=1),
            jnp.concatenate([imag, real], axis=1),
        ],
        axis=0,
    )


def swap_plane(plane, q, per):
    rows, lanes = plane.shape
    stride = per << q
    rolled = pltpu.roll(plane, lanes // 2, 1)
    low = lax.broadcasted_iota(jnp.int32, (stride, lanes), 1) < lanes // 2
    blocks = []
    for start in range(0, rows, 2 * stride):
        mid, end = start + stride, start + 2 * stride
        blocks.append(jnp.where(low, plane[start:mid], rolled[mid:end]))
        blocks.append(jnp.where(low, rolled[start:mid], plane[mid:end]))
    return jnp.concatenate(blocks, axis=0)


def swap(x, q, per):
    lanes = x.shape[1] // 2
    return jnp.concatenate(
        [swap_plane(x[:, :lanes], q, per), swap_plane(x[:, lanes:], q, per)], axis=1
    )


def polar(x, sweeps):
    gate = x.shape[0]
    norm = lax.rsqrt(jnp.sum(x * x, keepdims=True) + 1e-06)

    def sweep(_, a):
        high, low = split(a)

        def embed(v):
            real, imag = v[:, :gate], v[:, gate:]
            return jnp.concatenate([v, jnp.concatenate([-imag, real], axis=1)], axis=0)

        full = (embed(high), embed(low))
        def product(left, axis):
            def dot(u, v):
                return lax.dot_general(
                    u, v, (((1,), (axis,)), ((), ())), preferred_element_type=jnp.float32
                )

            both = dot(jnp.concatenate(left, axis=0), full[0])
            return both[:gate] + (both[gate:] + dot(left[0], full[1]))

        gram = product((high, low), 1)
        return 1.5 * a - 0.5 * product(split(gram), 0)

    return lax.fori_loop(0, sweeps, sweep, x * norm, unroll=8)


def kernel(
    used, order, extra_bits,
    psi_in, adj_in, gates_in, psi_out, adj_out,
    psi_buf, adj_buf, gates, phi_t, psi_send, adj_send,
    part, rs_buf, ag_buf, mid_buf,
    send_sem, recv_sem, local_sem,
):
    group = lax.axis_index("groups")
    me = lax.axis_index("long")
    n = 2 ** len(used)
    extra = 2 ** len(extra_bits)
    rows = psi_in.shape[1]
    gate = psi_in.shape[2]
    owners = n // 2
    first = n // 4
    own = gate // owners
    per = rows // owners

    def gather(value, bits):
        out = 0
        for k, bit in enumerate(bits):
            out = out + lax.rem(lax.div(value, 2**bit), 2) * 2**k
        return out

    def scatter(value, bits):
        out = 0
        for k, bit in enumerate(bits):
            out = out + lax.rem(lax.div(value, 2**k), 2) * 2**bit
        return out

    slot = gather(me, used)
    layer = gather(me, extra_bits)

    def peer(j):
        return scatter(j, used) + scatter(layer, extra_bits)

    def layer_peer(j):
        return scatter(slot, used) + scatter(j, extra_bits)

    def others(fn, mine=slot, count=n):
        def step(off, carry):
            fn(lax.rem(mine + off, count))
            return carry

        lax.fori_loop(1, count, step, 0)

    quarter = n // 4
    column = lax.div(slot, quarter)
    upper = lax.div(column, 2)
    inner = column + upper * (3 - 2 * column)

    def far_first(fn, ranks=(0, 1, 2, 3)):
        for rank in ranks:
            place = (3, 2, 1 - inner, inner)[rank]
            base = (place + upper * (3 - 2 * place)) * quarter

            def step(k, carry):
                fn(base + lax.rem(slot + 1 + k, quarter))
                return carry

            lax.fori_loop(0, quarter - (rank == 3), step, 0)

    def owners_far_first(fn, among=False):
        for rank in range(2):
            base = (2 - rank + upper * (2 * rank - 1)) * quarter

            def step(k, carry):
                fn(base + lax.rem(slot + 1 + k, quarter))
                return carry

            lax.fori_loop(0, quarter - rank, step, 0)

            if rank == 1 and not among:

                @pl.when(jnp.logical_not(is_owner))
                def _():
                    fn(base + lax.rem(slot, quarter))

    is_owner = inner == 1

    def remote(src, dst, phase, there, here, target):
        return pltpu.make_async_remote_copy(
            src_ref=src,
            dst_ref=dst,
            send_sem=send_sem.at[phase, there],
            recv_sem=recv_sem.at[phase, here],
            device_id={"groups": group, "long": target},
            device_id_type=MESH,
        )

    def block(ref, j, size):
        return ref.at[:, pl.ds(pl.multiple_of(j * size, size), size), :]

    index = slot - first

    def signal(j, target):
        pl.semaphore_signal(
            barrier, inc=1, device_id={"groups": group, "long": target(j)}, device_id_type=MESH
        )

    barrier = pltpu.get_barrier_semaphore()

    @pl.when(is_owner)
    def _():
        far_first(lambda j: signal(j, peer))
        if extra > 1:
            others(lambda j: signal(j, layer_peer), layer, extra)
        pl.semaphore_wait(barrier, n + extra - 2)

    @pl.when(jnp.logical_not(is_owner))
    def _():
        owners_far_first(lambda j: signal(j, peer))
        pl.semaphore_wait(barrier, owners)

    def inward(src, dst, phase):
        return lambda j: remote(
            block(src, j - first, per), block(dst, slot, per), phase, j, slot, peer(j)
        )

    def inward_from(dst, phase):
        return lambda j: remote(block(dst, j, per), block(dst, j, per), phase, j, j, peer(j))

    def outward(src, dst, phase):
        return lambda j: remote(
            block(src, j, per), block(dst, index, per), phase, j, slot, peer(j)
        )

    def outward_from(dst, phase):
        return lambda j: remote(
            block(dst, j - first, per), block(dst, j - first, per), phase, j, j, peer(j)
        )

    owners_far_first(lambda j: inward(adj_in, adj_buf, ADJ_IN)(j).start())
    owners_far_first(lambda j: inward(psi_in, psi_buf, PSI_IN)(j).start())

    def joined(ref):
        return jnp.concatenate([ref[0], ref[1]], axis=1)

    def put(ref, x):
        for q in order[::-1]:
            x = swap(x, q, per)
        ref[0] = x[:, :gate]
        ref[1] = x[:, gate:]

    def advance_adjoint(phi, s):
        full = split(embed_out(gates[s, 0], gates[s, 1]))
        phi = dot3(split(phi), full, ((1,), (1,)))
        high, low = split(phi.T)
        phi_t[s, 0] = high
        phi_t[s, 1] = low
        return phi

    @pl.when(is_owner)
    def _():
        gate_copy = pltpu.make_async_copy(gates_in, gates, local_sem.at[0])
        adj_own = pltpu.make_async_copy(block(adj_in, index, per), block(adj_buf, slot, per), local_sem.at[1])
        psi_own = pltpu.make_async_copy(block(psi_in, index, per), block(psi_buf, slot, per), local_sem.at[2])
        gate_copy.start()
        adj_own.start()
        psi_own.start()
        mine = pl.ds(pl.multiple_of(index * own, own), own)

        gate_copy.wait()
        adj_own.wait()
        others(lambda j: inward_from(adj_buf, ADJ_IN)(j).wait_recv())
        phi = joined(adj_buf)
        for s in range(SECTIONS):
            phi = advance_adjoint(swap(phi, order[s], per), s)
        put(adj_send, phi)
        adj_back = pltpu.make_async_copy(block(adj_send, slot, per), block(adj_out, index, per), local_sem.at[1])
        adj_back.start()
        psi_own.wait()
        others(lambda j: inward_from(psi_buf, PSI_IN)(j).wait_recv())
        psi = swap(joined(psi_buf), order[0], per)

        for s in range(SECTIONS):
            state = split(psi)
            outer = dot3((phi_t[s, 0], phi_t[s, 1]), state, ((1,), (0,)))
            part[s, 0] = outer[:gate, :gate] + outer[gate:, gate:]
            part[s, 1] = outer[gate:, :gate] - outer[:gate, gate:]

            def to_owner(j):
                return remote(
                    block(part.at[s], j - first, own), rs_buf.at[s, index], RS + s, j, slot, peer(j)
                )

            def from_owner(j):
                held = rs_buf.at[s, j - first]
                return remote(held, held, RS + s, j, j, peer(j))

            owners_far_first(lambda j: to_owner(j).start(), True)
            owners_far_first(lambda j: from_owner(j).wait_recv(), True)
            rs_buf[s, index] = part[s, :, mine, :]
            total = rs_buf[s, 0]
            for j in range(1, owners):
                total = total + rs_buf[s, j]
            if extra > 1:
                mid_buf[s, layer] = total

                def across(j, here):
                    held = mid_buf.at[s, here]
                    return remote(held, held, MID + s, j, here, layer_peer(j))

                others(lambda j: across(j, layer).start(), layer, extra)
                others(lambda j: across(j, j).wait_recv(), layer, extra)
                total = mid_buf[s, 0]
                for j in range(1, extra):
                    total = total + mid_buf[s, j]
            ag_buf[s, :, mine, :] = total
            held = block(ag_buf.at[s], index, own)
            owners_far_first(lambda j: remote(held, held, AG + s, j, slot, peer(j)).start(), True)

            def arrive(j):
                there = block(ag_buf.at[s], j - first, own)
                remote(there, there, AG + s, j, j, peer(j)).wait_recv()

            owners_far_first(arrive, True)
            if s < 3:
                back_ranks = ((2, 3), (0,), (1,))[s]
                far_first(lambda j: outward(adj_send, adj_out, ADJ_OUT)(j).start(), back_ranks)
            fitted = polar(jnp.concatenate([ag_buf[s, 0], ag_buf[s, 1]], axis=1), NS_ITERS)
            full = split(embed_out(fitted[:, :gate], fitted[:, gate:]))
            psi = dot3(state, full, ((1,), (1,)))
            if s + 1 < SECTIONS:
                psi = swap(psi, order[s + 1], per)

        put(psi_send, psi)
        far_first(lambda j: outward(psi_send, psi_out, PSI_OUT)(j).start())
        psi_back = pltpu.make_async_copy(block(psi_send, slot, per), block(psi_out, index, per), local_sem.at[2])
        psi_back.start()
        for s in range(SECTIONS):
            owners_far_first(
                lambda j: remote(block(part.at[s], j - first, own), rs_buf.at[s, index], RS + s, j, slot, peer(j)).wait_send(),
                True,
            )
            sent = block(ag_buf.at[s], index, own)
            owners_far_first(lambda j: remote(sent, sent, AG + s, j, slot, peer(j)).wait_send(), True)
            if extra > 1:
                done = mid_buf.at[s, layer]
                others(lambda j: remote(done, done, MID + s, j, layer, layer_peer(j)).wait_send(), layer, extra)
        adj_back.wait()
        psi_back.wait()
        others(lambda j: outward(adj_send, adj_out, ADJ_OUT)(j).wait_send())
        others(lambda j: outward(psi_send, psi_out, PSI_OUT)(j).wait_send())

    owners_far_first(lambda j: inward(adj_in, adj_buf, ADJ_IN)(j).wait_send())
    owners_far_first(lambda j: inward(psi_in, psi_buf, PSI_IN)(j).wait_send())
    owners_far_first(lambda j: outward_from(adj_out, ADJ_OUT)(j).wait_recv())
    owners_far_first(lambda j: outward_from(psi_out, PSI_OUT)(j).wait_recv())


def shards(initial_state, adjoint_state, current_gates):
    bit_count = lax.axis_size("long").bit_length() - 1
    partner_bits = [bit_count - 1, bit_count // 2, 0, 1]
    used = sorted(set(partner_bits))
    assert len(used) == SECTIONS
    order = [used.index(bit) for bit in partner_bits]
    extra_bits = [bit for bit in range(bit_count) if bit not in used]
    n, extra = 2 ** len(used), 2 ** len(extra_bits)
    planes, rows, gate = initial_state.shape
    owners = n // 2
    own = gate // owners
    held = n * (rows // owners)
    f32, bf16 = jnp.float32, jnp.bfloat16
    anywhere = pl.BlockSpec(memory_space=pl.ANY)
    return tuple(
        pl.pallas_call(
            functools.partial(kernel, used, order, extra_bits),
            out_shape=[pltpu.VMEM(initial_state.shape, f32)] * 2,
            in_specs=[anywhere] * 3,
            out_specs=[pl.BlockSpec(memory_space=pltpu.VMEM)] * 2,
            scratch_shapes=[
                pltpu.VMEM((2, held, gate), f32),
                pltpu.VMEM((2, held, gate), f32),
                pltpu.VMEM(current_gates.shape, f32),
                pltpu.VMEM((SECTIONS, 2, 2 * gate, held), bf16),
                pltpu.VMEM((2, held, gate), f32),
                pltpu.VMEM((2, held, gate), f32),
                pltpu.VMEM((SECTIONS, 2, gate, gate), f32),
                pltpu.VMEM((SECTIONS, owners, 2, own, gate), f32),
                pltpu.VMEM((SECTIONS, 2, gate, gate), f32),
                pltpu.VMEM((SECTIONS, extra, 2, own, gate), f32),
                pltpu.SemaphoreType.DMA((16, max(n, extra))),
                pltpu.SemaphoreType.DMA((16, max(n, extra))),
                pltpu.SemaphoreType.DMA((3,)),
            ],
            compiler_params=pltpu.CompilerParams(collective_id=0, has_side_effects=True),
            name="sweep",
        )(initial_state, adjoint_state, current_gates)
    )


def solution(mesh):
    return jax.shard_map(
        shards,
        mesh=mesh,
        in_specs=(
            P(None, ("groups", "long"), None),
            P(None, ("groups", "long"), None),
            P("groups", None, None, None),
        ),
        out_specs=(P(None, ("groups", "long"), None), P(None, ("groups", "long"), None)),
        check_vma=False,
    )
```

profile of v0, /device:TPU:0, one launch (start us, length us, event | category | flops | bytes accessed | tf_op | source)
XLA Modules:
  0.0 81.3 jit_solution(6341042193951143273)
XLA Ops:
  0.6 79.3 %sweep.1 = (f32[2,256,128]{2,1,0:T(8,128)S(1)}, f32[2,256,128]{2,1,0:T(8,128)S(1)}) custom-call(f32[2,256,128]{2,1,0:T(8,128)} %psi_in.1, f32[2,256,128]{2,1,0:T(8,128)} %adj_in.1, f32[4,2,128,128]{3,2,1,0:T(8,128)} %gates_in.1), custom_call_target="tpu_custom_call" | custom-call | tf_op jit(solution)/shard_map/sweep/pallas_call | solution.py:353
  79.9 0.7 copy.7
  80.6 0.7 copy.8
where the time goes:
time: 81.5 us; the launch traced here: 81.3 us
  Pallas kernels  79.3 us (97%)
  local copies, waits for them, and re-layouts  1.41 us (2%)
    pallas_call x1, Pallas kernels, shards(): pl.pallas_call(functools.partial(kernel, used, order, extra_bits), out_sh...  79.3 us

commit v1 on v0

v1 whole, which is shorter than its diff:
```python
import functools

import jax
import jax.numpy as jnp
from jax import lax
from jax.experimental import pallas as pl
from jax.experimental.pallas import tpu as pltpu
from jax.sharding import PartitionSpec as P

SECTIONS = 4
NS_ITERS = 8
MESH = pl.DeviceIdType.MESH
ADJ_IN, PSI_IN, ADJ_OUT, PSI_OUT, RS, AG, CROSS, MID = 0, 1, 2, 3, 4, 8, 12, 14
PHASES = 14
CHAINED = ()
BACK = ((2, 3), (0,), (1,), ())


def split(x):
    high = x.astype(jnp.bfloat16)
    return high, (x - high.astype(jnp.float32)).astype(jnp.bfloat16)


def dot3(left, right, contract):
    def dot(a, b):
        return lax.dot_general(
            a, b, (contract, ((), ())), preferred_element_type=jnp.float32
        )

    return dot(left[0], right[0]) + (dot(left[0], right[1]) + dot(left[1], right[0]))


def embed_out(real, imag):
    return jnp.concatenate(
        [
            jnp.concatenate([real, -imag], axis=1),
            jnp.concatenate([imag, real], axis=1),
        ],
        axis=0,
    )


def swap_plane(plane, q, per):
    rows, lanes = plane.shape
    stride = per << q
    rolled = pltpu.roll(plane, lanes // 2, 1)
    low = lax.broadcasted_iota(jnp.int32, (stride, lanes), 1) < lanes // 2
    blocks = []
    for start in range(0, rows, 2 * stride):
        mid, end = start + stride, start + 2 * stride
        blocks.append(jnp.where(low, plane[start:mid], rolled[mid:end]))
        blocks.append(jnp.where(low, rolled[start:mid], plane[mid:end]))
    return jnp.concatenate(blocks, axis=0)


def halves(x, q, per):
    stride = per << q
    starts = range(0, x.shape[0], 2 * stride)
    return [
        jnp.concatenate([x[k + bit * stride : k + (bit + 1) * stride] for k in starts], axis=0)
        for bit in range(2)
    ]


def swap(x, q, per):
    lanes = x.shape[1] // 2
    return jnp.concatenate(
        [swap_plane(x[:, :lanes], q, per), swap_plane(x[:, lanes:], q, per)], axis=1
    )


def embed(v):
    gate = v.shape[0]
    real, imag = v[:, :gate], v[:, gate:]
    return jnp.concatenate([v, jnp.concatenate([-imag, real], axis=1)], axis=0)


def contract_cross(cross, fitted):
    rows, gate = cross[0].shape
    half = gate // 2
    left = jnp.concatenate(
        [
            jnp.concatenate([cross[4 * u + 2 * v + plane] for u in range(2) for plane in range(2)], axis=1)
            for v in range(2)
        ],
        axis=0,
    )
    full = tuple(embed(x) for x in split(fitted))
    right = tuple(
        jnp.concatenate(
            [
                jnp.concatenate([x[u * half : (u + 1) * half], x[gate + u * half : gate + (u + 1) * half]], axis=0)
                for u in range(2)
            ],
            axis=1,
        )
        for x in full
    )
    out = dot3(split(left), right, ((1,), (1,)))
    low, high = out[:rows], out[rows:]
    return (
        jnp.concatenate([low[:, :half], high[:, :half]], axis=1),
        jnp.concatenate([low[:, half:], high[:, half:]], axis=1),
    )


def polar(x, sweeps):
    gate = x.shape[0]
    norm = lax.rsqrt(jnp.sum(x * x, keepdims=True) + 1e-06)

    def sweep(_, a):
        high, low = split(a)

        full = (embed(high), embed(low))
        def product(left, axis):
            def dot(u, v):
                return lax.dot_general(
                    u, v, (((1,), (axis,)), ((), ())), preferred_element_type=jnp.float32
                )

            both = dot(jnp.concatenate(left, axis=0), full[0])
            return both[:gate] + (both[gate:] + dot(left[0], full[1]))

        gram = product((high, low), 1)
        return 1.5 * a - 0.5 * product(split(gram), 0)

    return lax.fori_loop(0, sweeps, sweep, x * norm, unroll=8)


def kernel(
    used, order, extra_bits,
    psi_in, adj_in, gates_in, psi_out, adj_out,
    psi_buf, adj_buf, gates, phi_t, phi_cross, psi_send, adj_send,
    part, rs_buf, cross, cross_buf, ag_buf, mid_buf, mid_cross,
    send_sem, recv_sem, mid_send, mid_recv, local_sem,
):
    group = lax.axis_index("groups")
    me = lax.axis_index("long")
    n = 2 ** len(used)
    extra = 2 ** len(extra_bits)
    rows = psi_in.shape[1]
    gate = psi_in.shape[2]
    owners = n // 2
    first = n // 4
    own = gate // owners
    per = rows // owners

    def gather(value, bits):
        out = 0
        for k, bit in enumerate(bits):
            out = out + lax.rem(lax.div(value, 2**bit), 2) * 2**k
        return out

    def scatter(value, bits):
        out = 0
        for k, bit in enumerate(bits):
            out = out + lax.rem(lax.div(value, 2**k), 2) * 2**bit
        return out

    slot = gather(me, used)
    layer = gather(me, extra_bits)

    def peer(j):
        return scatter(j, used) + scatter(layer, extra_bits)

    def layer_peer(j):
        return scatter(slot, used) + scatter(j, extra_bits)

    def others(fn, mine=slot, count=n):
        def step(off, carry):
            fn(lax.rem(mine + off, count))
            return carry

        lax.fori_loop(1, count, step, 0)

    quarter = n // 4
    column = lax.div(slot, quarter)
    upper = lax.div(column, 2)
    inner = column + upper * (3 - 2 * column)

    def far_first(fn, ranks=(0, 1, 2, 3)):
        for rank in ranks:
            place = (3, 2, 1 - inner, inner)[rank]
            base = (place + upper * (3 - 2 * place)) * quarter

            def step(k, carry):
                fn(base + lax.rem(slot + 1 + k, quarter))
                return carry

            lax.fori_loop(0, quarter - (rank == 3), step, 0)

    def owners_far_first(fn, among=False):
        for rank in range(2):
            base = (2 - rank + upper * (2 * rank - 1)) * quarter

            def step(k, carry):
                fn(base + lax.rem(slot + 1 + k, quarter))
                return carry

            lax.fori_loop(0, quarter - rank, step, 0)

            if rank == 1 and not among:

                @pl.when(jnp.logical_not(is_owner))
                def _():
                    fn(base + lax.rem(slot, quarter))

    is_owner = inner == 1

    def remote(src, dst, phase, target):
        return pltpu.make_async_remote_copy(
            src_ref=src,
            dst_ref=dst,
            send_sem=send_sem.at[phase],
            recv_sem=recv_sem.at[phase],
            device_id={"groups": group, "long": target},
            device_id_type=MESH,
        )

    def block(ref, j, size):
        return ref.at[:, pl.ds(pl.multiple_of(j * size, size), size), :]

    def arrived(ref, phase):
        remote(ref, ref, phase, peer(lax.rem(slot + 1, n))).wait_recv()

    def departed(ref, phase):
        remote(ref, ref, phase, peer(lax.rem(slot + 1, n))).wait_send()

    index = slot - first

    def signal(j, target):
        pl.semaphore_signal(
            barrier, inc=1, device_id={"groups": group, "long": target(j)}, device_id_type=MESH
        )

    barrier = pltpu.get_barrier_semaphore()

    @pl.when(is_owner)
    def _():
        far_first(lambda j: signal(j, peer))
        if extra > 1:
            others(lambda j: signal(j, layer_peer), layer, extra)
        pl.semaphore_wait(barrier, n + extra - 2)

    @pl.when(jnp.logical_not(is_owner))
    def _():
        owners_far_first(lambda j: signal(j, peer))
        pl.semaphore_wait(barrier, owners)

    def inward(src, dst, phase):
        return lambda j: remote(block(src, j - first, per), block(dst, slot, per), phase, peer(j)).start()

    def outward(src, dst, phase):
        return lambda j: remote(block(src, j, per), block(dst, index, per), phase, peer(j)).start()

    owners_far_first(inward(adj_in, adj_buf, ADJ_IN))
    owners_far_first(inward(psi_in, psi_buf, PSI_IN))

    def joined(ref):
        return jnp.concatenate([ref[0], ref[1]], axis=1)

    def put(ref, x):
        for q in order[::-1]:
            x = swap(x, q, per)
        ref[0] = x[:, :gate]
        ref[1] = x[:, gate:]

    def advance_adjoint(phi, s):
        full = split(embed_out(gates[s, 0], gates[s, 1]))
        phi = dot3(split(phi), full, ((1,), (1,)))
        if s in CHAINED:
            for u, rows_u in enumerate(halves(phi, order[s], per)):
                high, low = split(rows_u.T)
                phi_cross[CHAINED.index(s), u, 0] = high
                phi_cross[CHAINED.index(s), u, 1] = low
        else:
            high, low = split(phi.T)
            phi_t[s, 0] = high
            phi_t[s, 1] = low
        return phi

    def outer(left, right):
        both = dot3(left, right, ((1,), (0,)))
        return both[:gate, :gate] + both[gate:, gate:], both[gate:, :gate] - both[:gate, gate:]

    def own_copy(src, dst, phase):
        return pltpu.make_async_copy(src, dst, recv_sem.at[phase])

    @pl.when(is_owner)
    def _():
        gate_copy = pltpu.make_async_copy(gates_in, gates, local_sem.at[0])
        gate_copy.start()
        own_copy(block(adj_in, index, per), block(adj_buf, slot, per), ADJ_IN).start()
        own_copy(block(psi_in, index, per), block(psi_buf, slot, per), PSI_IN).start()
        mine = pl.ds(pl.multiple_of(index * own, own), own)

        gate_copy.wait()
        arrived(adj_buf, ADJ_IN)
        phi = joined(adj_buf)
        for s in range(SECTIONS):
            phi = advance_adjoint(swap(phi, order[s], per), s)
        put(adj_send, phi)
        own_copy(block(adj_send, slot, per), block(adj_out, index, per), ADJ_OUT).start()
        adj_back = outward(adj_send, adj_out, ADJ_OUT)
        arrived(psi_buf, PSI_IN)
        psi = swap(joined(psi_buf), order[0], per)
        fitted = None

        def among(fn):
            owners_far_first(fn, True)

        def over_layers(buf, total, kind):
            buf[layer] = total

            def across(j, here):
                return pltpu.make_async_remote_copy(
                    src_ref=buf.at[here],
                    dst_ref=buf.at[here],
                    send_sem=mid_send.at[kind, j],
                    recv_sem=mid_recv.at[kind, here],
                    device_id={"groups": group, "long": layer_peer(j)},
                    device_id_type=MESH,
                )

            others(lambda j: across(j, layer).start(), layer, extra)
            others(lambda j: across(j, j).wait_recv(), layer, extra)
            others(lambda j: across(j, layer).wait_send(), layer, extra)
            total = buf[0]
            for j in range(1, extra):
                total = total + buf[j]
            return total

        def reduced(src, buf, phase):
            arrived(buf.at[pl.ds(0, owners - 1)], phase)
            buf[index] = src[:, mine, :]
            total = buf[0]
            for j in range(1, owners):
                total = total + buf[j]
            return total

        def send_cross(k, u):
            planes = pl.ds(4 * u, 4)
            among(
                lambda j: remote(
                    block(cross.at[k, planes], j - first, own), cross_buf.at[k, index, planes], CROSS + k, peer(j)
                ).start()
            )

        for s in range(SECTIONS):
            ahead = CHAINED.index(s + 1) if s + 1 in CHAINED else None
            state = split(psi)
            if s in CHAINED:
                k = CHAINED.index(s)
                total = reduced(cross.at[k], cross_buf.at[k], CROSS + k)
                if extra > 1:
                    total = over_layers(mid_cross.at[k], total, SECTIONS + k)
                ag_buf[s, 0, mine, :], ag_buf[s, 1, mine, :] = contract_cross(total, fitted)
            else:
                part[s, 0], part[s, 1] = outer((phi_t[s, 0], phi_t[s, 1]), state)
                among(
                    lambda j: remote(block(part.at[s], j - first, own), rs_buf.at[s, index], RS + s, peer(j)).start()
                )
                if ahead is not None:
                    for u in range(2):
                        for v in range(2):
                            right = tuple(halves(x, order[s + 1], per)[v] for x in state)
                            cross[ahead, 4 * u + 2 * v], cross[ahead, 4 * u + 2 * v + 1] = outer(
                                (phi_cross[ahead, u, 0], phi_cross[ahead, u, 1]), right
                            )
                        if u == 0:
                            send_cross(ahead, u)
                total = reduced(part.at[s], rs_buf.at[s], RS + s)
                if extra > 1:
                    total = over_layers(mid_buf.at[s], total, s)
                ag_buf[s, :, mine, :] = total
            held = block(ag_buf.at[s], index, own)
            among(lambda j: remote(held, held, AG + s, peer(j)).start())
            if s not in CHAINED and ahead is not None:
                send_cross(ahead, 1)
            if s in CHAINED:
                full = split(embed_out(fitted[:, :gate], fitted[:, gate:]))
                psi = swap(dot3(split(psi), full, ((1,), (1,))), order[s], per)
            for rank in BACK[s]:
                far_first(adj_back, (rank,))
            arrived(block(ag_buf.at[s], 0, (owners - 1) * own), AG + s)
            fitted = polar(jnp.concatenate([ag_buf[s, 0], ag_buf[s, 1]], axis=1), NS_ITERS)
            if ahead is None:
                full = split(embed_out(fitted[:, :gate], fitted[:, gate:]))
                psi = dot3(split(psi), full, ((1,), (1,)))
                if s + 1 < SECTIONS:
                    psi = swap(psi, order[s + 1], per)

        put(psi_send, psi)
        far_first(outward(psi_send, psi_out, PSI_OUT))
        own_copy(block(psi_send, slot, per), block(psi_out, index, per), PSI_OUT).start()
        for s in range(SECTIONS):
            sent = block(part.at[s], 0, (owners - 1) * own)
            departed(sent, AG + s)
            if s in CHAINED:
                k = CHAINED.index(s)
                departed(block(cross.at[k], 0, (owners - 1) * own), CROSS + k)
            else:
                departed(sent, RS + s)
        departed(block(adj_in, 0, (owners - 1) * per), ADJ_IN)
        departed(block(psi_in, 0, (owners - 1) * per), PSI_IN)
        departed(block(adj_send, 0, (n - 1) * per), ADJ_OUT)
        departed(block(psi_send, 0, (n - 1) * per), PSI_OUT)

    @pl.when(jnp.logical_not(is_owner))
    def _():
        departed(adj_in, ADJ_IN)
        departed(psi_in, PSI_IN)

    arrived(adj_out, ADJ_OUT)
    arrived(psi_out, PSI_OUT)


def shards(initial_state, adjoint_state, current_gates):
    bit_count = lax.axis_size("long").bit_length() - 1
    partner_bits = [bit_count - 1, bit_count // 2, 0, 1]
    used = sorted(set(partner_bits))
    assert len(used) == SECTIONS
    order = [used.index(bit) for bit in partner_bits]
    extra_bits = [bit for bit in range(bit_count) if bit not in used]
    n, extra = 2 ** len(used), 2 ** len(extra_bits)
    planes, rows, gate = initial_state.shape
    owners = n // 2
    own = gate // owners
    held = n * (rows // owners)
    f32, bf16 = jnp.float32, jnp.bfloat16
    anywhere = pl.BlockSpec(memory_space=pl.ANY)
    return tuple(
        pl.pallas_call(
            functools.partial(kernel, used, order, extra_bits),
            out_shape=[pltpu.VMEM(initial_state.shape, f32)] * 2,
            in_specs=[anywhere] * 3,
            out_specs=[pl.BlockSpec(memory_space=pltpu.VMEM)] * 2,
            scratch_shapes=[
                pltpu.VMEM((2, held, gate), f32),
                pltpu.VMEM((2, held, gate), f32),
                pltpu.VMEM(current_gates.shape, f32),
                pltpu.VMEM((SECTIONS, 2, 2 * gate, held), bf16),
                pltpu.VMEM((2, 2, 2, 2 * gate, held // 2), bf16),
                pltpu.VMEM((2, held, gate), f32),
                pltpu.VMEM((2, held, gate), f32),
                pltpu.VMEM((SECTIONS, 2, gate, gate), f32),
                pltpu.VMEM((SECTIONS, owners, 2, own, gate), f32),
                pltpu.VMEM((2, 8, gate, gate), f32),
                pltpu.VMEM((2, owners, 8, own, gate), f32),
                pltpu.VMEM((SECTIONS, 2, gate, gate), f32),
                pltpu.VMEM((SECTIONS, extra, 2, own, gate), f32),
                pltpu.VMEM((2, extra, 8, own, gate), f32),
                pltpu.SemaphoreType.DMA((PHASES,)),
                pltpu.SemaphoreType.DMA((PHASES,)),
                pltpu.SemaphoreType.DMA((SECTIONS + 2 if extra > 1 else 1, extra)),
                pltpu.SemaphoreType.DMA((SECTIONS + 2 if extra > 1 else 1, extra)),
                pltpu.SemaphoreType.DMA((1,)),
            ],
            compiler_params=pltpu.CompilerParams(collective_id=0, has_side_effects=True),
            name="sweep",
        )(initial_state, adjoint_state, current_gates)
    )


def solution(mesh):
    return jax.shard_map(
        shards,
        mesh=mesh,
        in_specs=(
            P(None, ("groups", "long"), None),
            P(None, ("groups", "long"), None),
            P("groups", None, None, None),
        ),
        out_specs=(P(None, ("groups", "long"), None), P(None, ("groups", "long"), None)),
        check_vma=False,
    )
```

time: 81.5 us -> 78.2 us (0.960)
  Pallas kernels: 79.3 us -> 76 us
    pallas_call x1, Pallas kernels: 79.3 us -> 76 us  [shards(): pl.pallas_call(functools.partial(kernel, used, order, extra_bits), out_sh...]
where the time goes in v1:
time: 78.2 us; the launch traced here: 78.1 us
  Pallas kernels  76 us (97%)
  local copies, waits for them, and re-layouts  1.41 us (2%)
    pallas_call x1, Pallas kernels, shards(): pl.pallas_call(functools.partial(kernel, used, order, extra_bits), out_sh...  76 us

profile of v1, /device:TPU:0, one launch (start us, length us, event | category | flops | bytes accessed | tf_op | source)
XLA Modules:
  0.0 78.1 jit_solution(10844506394094517349)
XLA Ops:
  0.6 76.0 %sweep.1 = (f32[2,256,128]{2,1,0:T(8,128)S(1)}, f32[2,256,128]{2,1,0:T(8,128)S(1)}) custom-call(f32[2,256,128]{2,1,0:T(8,128)} %psi_in.1, f32[2,256,128]{2,1,0:T(8,128)} %adj_in.1, f32[4,2,128,128]{3,2,1,0:T(8,128)} %gates_in.1), custom_call_target="tpu_custom_call" | custom-call | tf_op jit(solution)/shard_map/sweep/pallas_call | solution.py:433
  76.6 0.7 copy.7
  77.4 0.7 copy.8

commit v2 on v1

--- a/solution.py
+++ b/solution.py
@@ -12,8 +12,8 @@
 MESH = pl.DeviceIdType.MESH
 ADJ_IN, PSI_IN, ADJ_OUT, PSI_OUT, RS, AG, CROSS, MID = 0, 1, 2, 3, 4, 8, 12, 14
 PHASES = 14
-CHAINED = ()
-BACK = ((2, 3), (0,), (1,), ())
+CHAINED = (1, 3)
+BACK = ((), (0, 1, 2, 3), (), ())
 
 
 def split(x):

time: 78.2 us -> 71.5 us (0.914)
  Pallas kernels: 76 us -> 69.3 us
    pallas_call x1, Pallas kernels: 76 us -> 69.3 us  [shards(): pl.pallas_call(functools.partial(kernel, used, order, extra_bits), out_sh...]
where the time goes in v2:
time: 71.5 us; the launch traced here: 71.4 us
  Pallas kernels  69.3 us (97%)
  local copies, waits for them, and re-layouts  1.41 us (2%)
    pallas_call x1, Pallas kernels, shards(): pl.pallas_call(functools.partial(kernel, used, order, extra_bits), out_sh...  69.3 us

profile of v2, /device:TPU:0, one launch (start us, length us, event | category | flops | bytes accessed | tf_op | source)
XLA Modules:
  0.0 71.4 jit_solution(17590069341976378253)
XLA Ops:
  0.6 69.3 %sweep.1 = (f32[2,256,128]{2,1,0:T(8,128)S(1)}, f32[2,256,128]{2,1,0:T(8,128)S(1)}) custom-call(f32[2,256,128]{2,1,0:T(8,128)} %psi_in.1, f32[2,256,128]{2,1,0:T(8,128)} %adj_in.1, f32[4,2,128,128]{3,2,1,0:T(8,128)} %gates_in.1), custom_call_target="tpu_custom_call" | custom-call | tf_op jit(solution)/shard_map/sweep/pallas_call | solution.py:433
  70.0 0.7 copy.7
  70.7 0.7 copy.8

commit v3 on v2

--- a/solution.py
+++ b/solution.py
@@ -10,10 +10,12 @@
 SECTIONS = 4
 NS_ITERS = 8
 MESH = pl.DeviceIdType.MESH
-ADJ_IN, PSI_IN, ADJ_OUT, PSI_OUT, RS, AG, CROSS, MID = 0, 1, 2, 3, 4, 8, 12, 14
-PHASES = 14
+ADJ_IN, PSI_IN, ADJ_OUT, FAR, NEAR, HALF, FINAL, RS, AG, CROSS = 0, 1, 2, 3, 4, 5, 7, 11, 15, 19
 CHAINED = (1, 3)
-BACK = ((), (0, 1, 2, 3), (), ())
+CORE = CROSS + len(CHAINED)
+PHASES = CORE + 2 * len(CHAINED)
+BACK = ((), (0, 1, 2, 3), (), (), ())
+SEND = (((), ()), ((), ()), ((2, 3), (0, 1)), ((), ()))
 
 
 def split(x):
@@ -40,9 +42,8 @@
     )
 
 
-def swap_plane(plane, q, per):
+def swap_plane(plane, stride):
     rows, lanes = plane.shape
-    stride = per << q
     rolled = pltpu.roll(plane, lanes // 2, 1)
     low = lax.broadcasted_iota(jnp.int32, (stride, lanes), 1) < lanes // 2
     blocks = []
@@ -62,11 +63,15 @@
     ]
 
 
-def swap(x, q, per):
+def swap_rows(x, stride):
     lanes = x.shape[1] // 2
     return jnp.concatenate(
-        [swap_plane(x[:, :lanes], q, per), swap_plane(x[:, lanes:], q, per)], axis=1
+        [swap_plane(x[:, :lanes], stride), swap_plane(x[:, lanes:], stride)], axis=1
     )
+
+
+def swap(x, q, per):
+    return swap_rows(x, per << q)
 
 
 def embed(v):
@@ -131,7 +136,7 @@
     used, order, extra_bits,
     psi_in, adj_in, gates_in, psi_out, adj_out,
     psi_buf, adj_buf, gates, phi_t, phi_cross, psi_send, adj_send,
-    part, rs_buf, cross, cross_buf, ag_buf, mid_buf, mid_cross,
+    part, rs_buf, cross, pair_buf, chip_buf, cross_buf, ag_buf, final, half_gate, mid_buf, mid_cross,
     send_sem, recv_sem, mid_send, mid_recv, local_sem,
 ):
     group = lax.axis_index("groups")
@@ -157,11 +162,11 @@
             out = out + lax.rem(lax.div(value, 2**k), 2) * 2**bit
         return out
 
-    slot = gather(me, used)
+    slot = gather(me, used) if extra_bits else me
     layer = gather(me, extra_bits)
 
     def peer(j):
-        return scatter(j, used) + scatter(layer, extra_bits)
+        return scatter(j, used) + scatter(layer, extra_bits) if extra_bits else j
 
     def layer_peer(j):
         return scatter(slot, used) + scatter(j, extra_bits)
@@ -187,7 +192,8 @@
                 fn(base + lax.rem(slot + 1 + k, quarter))
                 return carry
 
-            lax.fori_loop(0, quarter - (rank == 3), step, 0)
+            for k in range(quarter - (rank == 3)):
+                step(k, 0)
 
     def owners_far_first(fn, among=False):
         for rank in range(2):
@@ -197,7 +203,8 @@
                 fn(base + lax.rem(slot + 1 + k, quarter))
                 return carry
 
-            lax.fori_loop(0, quarter - rank, step, 0)
+            for k in range(quarter - rank):
+                step(k, 0)
 
             if rank == 1 and not among:
 
@@ -228,6 +235,9 @@
 
     index = slot - first
 
+    def shard(k):
+        return lax.rem(k, 2) * (owners // 2) + lax.div(k, 2)
+
     def signal(j, target):
         pl.semaphore_signal(
             barrier, inc=1, device_id={"groups": group, "long": target(j)}, device_id_type=MESH
@@ -253,14 +263,82 @@
     def outward(src, dst, phase):
         return lambda j: remote(block(src, j, per), block(dst, index, per), phase, peer(j)).start()
 
+    def bit_of(q):
+        return lax.rem(lax.div(slot, 2**q), 2)
+
+    def flipped(q):
+        return peer(slot + (1 - 2 * bit_of(q)) * 2**q)
+
+    def variant(near, far):
+        return near + 2 * far
+
+    near_bit, far_bit = bit_of(order[2]), bit_of(order[3])
+    mine_at = variant(near_bit, far_bit)
+    other_at = variant(near_bit, 1 - far_bit)
+    chunks = owners // 2
+    chips = owners // 2
+    wide = gate // 2
+    pair = rows // chunks
+
+    def target_variant(j):
+        return variant(lax.rem(lax.div(j, 2 ** order[2]), 2), lax.rem(lax.div(j, 2 ** order[3]), 2))
+
+    def to_final(j):
+        remote(
+            block(psi_send, j, per),
+            block(final.at[target_variant(j)], index, per),
+            FINAL + lax.div(index, 2),
+            peer(j),
+        ).start()
+
+    def pass_across():
+        def step(k, carry):
+            part_k = lax.rem(k + upper * (chunks // 2), chunks)
+            ref = block(final.at[mine_at], part_k, pair)
+            arrived(ref, FINAL + part_k)
+            remote(ref, ref, FAR, flipped(order[3])).start()
+            return carry
+
+        lax.fori_loop(0, chunks, step, 0)
+        remote(final.at[mine_at], final.at[mine_at], NEAR, flipped(order[2])).start()
+
+    def gather_final():
+        arrived(final.at[other_at], FAR)
+        remote(final.at[other_at], final.at[other_at], NEAR, flipped(order[2])).start()
+        arrived(final.at[pl.ds(0, 2)], NEAR)
+
+    def keep_half(k, bit, x):
+        half = gate // 2
+        half_gate[k] = jnp.where(bit == 0, x[:half], x[half:])
+
+    def fit(s):
+        return polar(jnp.concatenate([ag_buf[s, 0], ag_buf[s, 1]], axis=1), NS_ITERS)
+
+    def half_apply(x, k):
+        full = embed_out(half_gate[k, :, :gate], half_gate[k, :, gate:])
+        return dot3(split(x), split(full), ((1,), (1,)))
+
+    def before_last():
+        outs = []
+        for far in range(2):
+            both = [joined(final.at[variant(near, far)]) for near in range(2)]
+            outs.append(half_apply(swap_rows(jnp.concatenate(both, axis=0), rows), 0))
+        x = swap_plane(jnp.concatenate(outs, axis=0), 2 * rows)
+        return jnp.concatenate([x[: 2 * rows], x[2 * rows :]], axis=1)
+
+    def last(x):
+        x = swap_plane(half_apply(x, 1), rows)
+        psi_out[0] = x[:rows]
+        psi_out[1] = x[rows:]
+
+    def joined(ref):
+        return jnp.concatenate([ref[0], ref[1]], axis=1)
+
     owners_far_first(inward(adj_in, adj_buf, ADJ_IN))
     owners_far_first(inward(psi_in, psi_buf, PSI_IN))
 
-    def joined(ref):
-        return jnp.concatenate([ref[0], ref[1]], axis=1)
-
-    def put(ref, x):
-        for q in order[::-1]:
+    def put(ref, x, done):
+        for q in done[::-1]:
             x = swap(x, q, per)
         ref[0] = x[:, :gate]
         ref[1] = x[:, gate:]
@@ -292,16 +370,20 @@
         gate_copy.start()
         own_copy(block(adj_in, index, per), block(adj_buf, slot, per), ADJ_IN).start()
         own_copy(block(psi_in, index, per), block(psi_buf, slot, per), PSI_IN).start()
-        mine = pl.ds(pl.multiple_of(index * own, own), own)
+        chip = lax.div(index, 2)
+        parity = lax.rem(index, 2)
+        mine = pl.ds(pl.multiple_of(shard(index) * own, own), own)
 
         gate_copy.wait()
         arrived(adj_buf, ADJ_IN)
         phi = joined(adj_buf)
         for s in range(SECTIONS):
             phi = advance_adjoint(swap(phi, order[s], per), s)
-        put(adj_send, phi)
+        put(adj_send, phi, order)
         own_copy(block(adj_send, slot, per), block(adj_out, index, per), ADJ_OUT).start()
         adj_back = outward(adj_send, adj_out, ADJ_OUT)
+        for rank in BACK[SECTIONS]:
+            far_first(adj_back, (rank,))
         arrived(psi_buf, PSI_IN)
         psi = swap(joined(psi_buf), order[0], per)
         fitted = None
@@ -340,79 +422,145 @@
 
         def send_cross(k, u):
             planes = pl.ds(4 * u, 4)
-            among(
-                lambda j: remote(
-                    block(cross.at[k, planes], j - first, own), cross_buf.at[k, index, planes], CROSS + k, peer(j)
+            remote(
+                block(cross.at[k, planes], 1 - parity, wide), pair_buf.at[k, planes], CORE + 2 * k + u, flipped(0)
+            ).start()
+
+        def pass_cross(k, u):
+            planes = pl.ds(4 * u, 4)
+            arrived(pair_buf.at[k, planes], CORE + 2 * k + u)
+            rows_here = pl.ds(pl.multiple_of(parity * wide, wide), wide)
+            chip_buf[k, planes] = cross[k, planes, rows_here, :] + pair_buf[k, planes]
+
+            def step(off, carry):
+                there = lax.rem(chip + off, chips)
+                remote(
+                    block(chip_buf.at[k, planes], there, own),
+                    cross_buf.at[k, chip, planes],
+                    CROSS + k,
+                    peer(first + 2 * there + parity),
                 ).start()
-            )
+                return carry
+
+            lax.fori_loop(1, chips, step, 0)
+
+        def reduced_cross(k):
+            arrived(cross_buf.at[k, pl.ds(0, chips - 1)], CROSS + k)
+            cross_buf[k, chip] = chip_buf[k, :, pl.ds(pl.multiple_of(chip * own, own), own), :]
+            total = cross_buf[k, 0]
+            for j in range(1, chips):
+                total = total + cross_buf[k, j]
+            return total
+
+        def send_plain(x):
+            put(psi_send, x, order[:3])
+            pltpu.make_async_copy(
+                block(psi_send, slot, per), block(final.at[mine_at], index, per), recv_sem.at[FINAL + lax.div(index, 2)]
+            ).start()
+
+        def fill_cross(k, s, x):
+            state = split(x)
+            for u in range(2):
+                for v in range(2):
+                    right = tuple(halves(h, order[s + 1], per)[v] for h in state)
+                    cross[k, 4 * u + 2 * v], cross[k, 4 * u + 2 * v + 1] = outer(
+                        (phi_cross[k, u, 0], phi_cross[k, u, 1]), right
+                    )
+                send_cross(k, u)
+            for u in range(2):
+                pass_cross(k, u)
+
+        def apply(x, gate_pair):
+            return dot3(split(x), split(embed_out(gate_pair[:, :gate], gate_pair[:, gate:])), ((1,), (1,)))
+
+        outer_peer = 3 * upper * quarter + lax.rem(slot, quarter)
+
+        def share_half(k, bit, x):
+            keep_half(k, bit, x)
+            if k == 0:
+                remote(half_gate.at[k], half_gate.at[k], HALF, peer(outer_peer)).start()
 
         for s in range(SECTIONS):
             ahead = CHAINED.index(s + 1) if s + 1 in CHAINED else None
-            state = split(psi)
             if s in CHAINED:
                 k = CHAINED.index(s)
-                total = reduced(cross.at[k], cross_buf.at[k], CROSS + k)
+                total = reduced_cross(k)
                 if extra > 1:
                     total = over_layers(mid_cross.at[k], total, SECTIONS + k)
                 ag_buf[s, 0, mine, :], ag_buf[s, 1, mine, :] = contract_cross(total, fitted)
             else:
-                part[s, 0], part[s, 1] = outer((phi_t[s, 0], phi_t[s, 1]), state)
+                part[s, 0], part[s, 1] = outer((phi_t[s, 0], phi_t[s, 1]), split(psi))
                 among(
-                    lambda j: remote(block(part.at[s], j - first, own), rs_buf.at[s, index], RS + s, peer(j)).start()
+                    lambda j: remote(block(part.at[s], shard(j - first), own), rs_buf.at[s, index], RS + s, peer(j)).start()
                 )
                 if ahead is not None:
-                    for u in range(2):
-                        for v in range(2):
-                            right = tuple(halves(x, order[s + 1], per)[v] for x in state)
-                            cross[ahead, 4 * u + 2 * v], cross[ahead, 4 * u + 2 * v + 1] = outer(
-                                (phi_cross[ahead, u, 0], phi_cross[ahead, u, 1]), right
-                            )
-                        if u == 0:
-                            send_cross(ahead, u)
+                    fill_cross(ahead, s, psi)
+                if s == 2:
+                    send_plain(psi)
+                for rank in SEND[s][0]:
+                    far_first(to_final, (rank,))
                 total = reduced(part.at[s], rs_buf.at[s], RS + s)
                 if extra > 1:
                     total = over_layers(mid_buf.at[s], total, s)
                 ag_buf[s, :, mine, :] = total
-            held = block(ag_buf.at[s], index, own)
+            held = block(ag_buf.at[s], shard(index), own)
             among(lambda j: remote(held, held, AG + s, peer(j)).start())
-            if s not in CHAINED and ahead is not None:
-                send_cross(ahead, 1)
-            if s in CHAINED:
-                full = split(embed_out(fitted[:, :gate], fitted[:, gate:]))
-                psi = swap(dot3(split(psi), full, ((1,), (1,))), order[s], per)
+            if s == SECTIONS - 1:
+                far_first(lambda j: remote(held, held, AG + s, peer(j)).start(), (0, 2))
+            if s in CHAINED and s < SECTIONS - 1:
+                psi = swap(apply(psi, fitted), order[s], per)
+                if ahead is not None:
+                    fill_cross(ahead, s, psi)
+                if s == 2:
+                    send_plain(psi)
             for rank in BACK[s]:
                 far_first(adj_back, (rank,))
+            for rank in SEND[s][1]:
+                far_first(to_final, (rank,))
+            if s == SECTIONS - 1:
+                pass_across()
             arrived(block(ag_buf.at[s], 0, (owners - 1) * own), AG + s)
-            fitted = polar(jnp.concatenate([ag_buf[s, 0], ag_buf[s, 1]], axis=1), NS_ITERS)
-            if ahead is None:
-                full = split(embed_out(fitted[:, :gate], fitted[:, gate:]))
-                psi = dot3(split(psi), full, ((1,), (1,)))
-                if s + 1 < SECTIONS:
-                    psi = swap(psi, order[s + 1], per)
-
-        put(psi_send, psi)
-        far_first(outward(psi_send, psi_out, PSI_OUT))
-        own_copy(block(psi_send, slot, per), block(psi_out, index, per), PSI_OUT).start()
+            fitted = fit(s)
+            if s == SECTIONS - 2:
+                share_half(0, near_bit, fitted)
+            if s == SECTIONS - 1:
+                share_half(1, far_bit, fitted)
+            if ahead is None and s < SECTIONS - 1:
+                psi = swap(apply(psi, fitted), order[s + 1], per)
+
+        gather_final()
+        last(before_last())
         for s in range(SECTIONS):
             sent = block(part.at[s], 0, (owners - 1) * own)
-            departed(sent, AG + s)
+            departed(block(psi_send, 0, (n - 1) * own) if s == SECTIONS - 1 else sent, AG + s)
             if s in CHAINED:
                 k = CHAINED.index(s)
-                departed(block(cross.at[k], 0, (owners - 1) * own), CROSS + k)
+                departed(block(chip_buf.at[k], 0, (chips - 1) * own), CROSS + k)
+                for u in range(2):
+                    departed(pair_buf.at[k, pl.ds(4 * u, 4)], CORE + 2 * k + u)
             else:
                 departed(sent, RS + s)
         departed(block(adj_in, 0, (owners - 1) * per), ADJ_IN)
         departed(block(psi_in, 0, (owners - 1) * per), PSI_IN)
         departed(block(adj_send, 0, (n - 1) * per), ADJ_OUT)
-        departed(block(psi_send, 0, (n - 1) * per), PSI_OUT)
+        departed(block(psi_send, 0, (n - 1) * per), FINAL + lax.div(index, 2))
+        departed(half_gate.at[0], HALF)
 
     @pl.when(jnp.logical_not(is_owner))
     def _():
+        pass_across()
+        gather_final()
+        arrived(half_gate.at[0], HALF)
+        x = before_last()
+        arrived(ag_buf.at[SECTIONS - 1], AG + SECTIONS - 1)
+        keep_half(1, far_bit, fit(SECTIONS - 1))
+        last(x)
         departed(adj_in, ADJ_IN)
         departed(psi_in, PSI_IN)
 
+    departed(final.at[mine_at], FAR)
+    departed(final.at[pl.ds(0, 2)], NEAR)
     arrived(adj_out, ADJ_OUT)
-    arrived(psi_out, PSI_OUT)
 
 
 def shards(initial_state, adjoint_state, current_gates):
@@ -440,20 +588,24 @@
                 pltpu.VMEM((2, held, gate), f32),
                 pltpu.VMEM(current_gates.shape, f32),
                 pltpu.VMEM((SECTIONS, 2, 2 * gate, held), bf16),
-                pltpu.VMEM((2, 2, 2, 2 * gate, held // 2), bf16),
+                pltpu.VMEM((len(CHAINED), 2, 2, 2 * gate, held // 2), bf16),
                 pltpu.VMEM((2, held, gate), f32),
                 pltpu.VMEM((2, held, gate), f32),
                 pltpu.VMEM((SECTIONS, 2, gate, gate), f32),
                 pltpu.VMEM((SECTIONS, owners, 2, own, gate), f32),
-                pltpu.VMEM((2, 8, gate, gate), f32),
-                pltpu.VMEM((2, owners, 8, own, gate), f32),
+                pltpu.VMEM((len(CHAINED), 8, gate, gate), f32),
+                pltpu.VMEM((len(CHAINED), 8, gate // 2, gate), f32),
+                pltpu.VMEM((len(CHAINED), 8, gate // 2, gate), f32),
+                pltpu.VMEM((len(CHAINED), owners // 2, 8, own, gate), f32),
                 pltpu.VMEM((SECTIONS, 2, gate, gate), f32),
+                pltpu.VMEM((4, planes, rows, gate), f32),
+                pltpu.VMEM((2, gate // 2, 2 * gate), f32),
                 pltpu.VMEM((SECTIONS, extra, 2, own, gate), f32),
-                pltpu.VMEM((2, extra, 8, own, gate), f32),
+                pltpu.VMEM((len(CHAINED), extra, 8, own, gate), f32),
                 pltpu.SemaphoreType.DMA((PHASES,)),
                 pltpu.SemaphoreType.DMA((PHASES,)),
-                pltpu.SemaphoreType.DMA((SECTIONS + 2 if extra > 1 else 1, extra)),
-                pltpu.SemaphoreType.DMA((SECTIONS + 2 if extra > 1 else 1, extra)),
+                pltpu.SemaphoreType.DMA((SECTIONS + len(CHAINED) if extra > 1 else 1, extra)),
+                pltpu.SemaphoreType.DMA((SECTIONS + len(CHAINED) if extra > 1 else 1, extra)),
                 pltpu.SemaphoreType.DMA((1,)),
             ],
             compiler_params=pltpu.CompilerParams(collective_id=0, has_side_effects=True),

time: 71.5 us -> 66.4 us (0.929)
  Pallas kernels: 69.3 us -> 64.2 us
    pallas_call x1, Pallas kernels: 69.3 us -> 64.2 us  [shards(): pl.pallas_call(functools.partial(kernel, used, order, extra_bits), out_sh...]
where the time goes in v3:
time: 66.4 us; the launch traced here: 66.2 us
  Pallas kernels  64.2 us (97%)
  local copies, waits for them, and re-layouts  1.41 us (2%)
    pallas_call x1, Pallas kernels, shards(): pl.pallas_call(functools.partial(kernel, used, order, extra_bits), out_sh...  64.2 us
    unnamed x2, local copies, waits for them, and re-layouts  1.41 us

profile of v3, /device:TPU:0, one launch (start us, length us, event | category | flops | bytes accessed | tf_op | source)
XLA Modules:
  0.0 66.2 jit_solution(17661784011508454825)
XLA Ops:
  0.6 64.2 %sweep.1 = (f32[2,256,128]{2,1,0:T(8,128)S(1)}, f32[2,256,128]{2,1,0:T(8,128)S(1)}) custom-call(f32[2,256,128]{2,1,0:T(8,128)} %psi_in.1, f32[2,256,128]{2,1,0:T(8,128)} %adj_in.1, f32[4,2,128,128]{3,2,1,0:T(8,128)} %gates_in.1), custom_call_target="tpu_custom_call" | custom-call | tf_op jit(solution)/shard_map/sweep/pallas_call | solution.py:581
  64.8 0.7 %copy.7 = f32[2,256,128]{2,1,0:T(8,128)} copy(f32[2,256,128]{2,1,0:T(8,128)S(1)} %get-tuple-element.2) | data formatting | bytes 524288
  65.5 0.7 %copy.8 = f32[2,256,128]{2,1,0:T(8,128)} copy(f32[2,256,128]{2,1,0:T(8,128)S(1)} %get-tuple-element.3) | data formatting | bytes 524288

commit v4 on v3

--- a/solution.py
+++ b/solution.py
@@ -10,11 +10,11 @@
 SECTIONS = 4
 NS_ITERS = 8
 MESH = pl.DeviceIdType.MESH
-ADJ_IN, PSI_IN, ADJ_OUT, FAR, NEAR, HALF, FINAL, RS, AG, CROSS = 0, 1, 2, 3, 4, 5, 7, 11, 15, 19
-CHAINED = (1, 3)
+ADJ_IN, PSI_IN, ADJ_OUT, NEAR, HALF, FAR, FINAL, RS, AG, CROSS = 0, 1, 2, 3, 4, 5, 9, 17, 21, 25
+CHAINED = (1, 2, 3)
 CORE = CROSS + len(CHAINED)
 PHASES = CORE + 2 * len(CHAINED)
-BACK = ((), (0, 1, 2, 3), (), (), ())
+BACK = ((0, 1), (), (), (), (2, 3))
 SEND = (((), ()), ((), ()), ((2, 3), (0, 1)), ((), ()))
 
 
@@ -250,11 +250,10 @@
         far_first(lambda j: signal(j, peer))
         if extra > 1:
             others(lambda j: signal(j, layer_peer), layer, extra)
-        pl.semaphore_wait(barrier, n + extra - 2)
+        pl.semaphore_wait(barrier, owners + extra - 2)
 
     @pl.when(jnp.logical_not(is_owner))
     def _():
-        owners_far_first(lambda j: signal(j, peer))
         pl.semaphore_wait(barrier, owners)
 
     def inward(src, dst, phase):
@@ -287,24 +286,30 @@
         remote(
             block(psi_send, j, per),
             block(final.at[target_variant(j)], index, per),
-            FINAL + lax.div(index, 2),
+            FINAL + index,
             peer(j),
         ).start()
 
     def pass_across():
         def step(k, carry):
+            part_k = lax.rem(k + upper * (owners // 2), owners)
+            ref = block(final.at[mine_at], part_k, per)
+            arrived(ref, FINAL + part_k)
+            remote(ref, ref, FAR + lax.div(part_k, 2), flipped(order[3])).start()
+            remote(ref, ref, NEAR, flipped(order[2])).start()
+            return carry
+
+        lax.fori_loop(0, owners, step, 0)
+
+    def gather_final():
+        def step(k, carry):
             part_k = lax.rem(k + upper * (chunks // 2), chunks)
-            ref = block(final.at[mine_at], part_k, pair)
-            arrived(ref, FINAL + part_k)
-            remote(ref, ref, FAR, flipped(order[3])).start()
+            ref = block(final.at[other_at], part_k, pair)
+            arrived(ref, FAR + part_k)
+            remote(ref, ref, NEAR, flipped(order[2])).start()
             return carry
 
         lax.fori_loop(0, chunks, step, 0)
-        remote(final.at[mine_at], final.at[mine_at], NEAR, flipped(order[2])).start()
-
-    def gather_final():
-        arrived(final.at[other_at], FAR)
-        remote(final.at[other_at], final.at[other_at], NEAR, flipped(order[2])).start()
         arrived(final.at[pl.ds(0, 2)], NEAR)
 
     def keep_half(k, bit, x):
@@ -452,10 +457,10 @@
                 total = total + cross_buf[k, j]
             return total
 
-        def send_plain(x):
-            put(psi_send, x, order[:3])
+        def send_plain(x, done):
+            put(psi_send, x, done)
             pltpu.make_async_copy(
-                block(psi_send, slot, per), block(final.at[mine_at], index, per), recv_sem.at[FINAL + lax.div(index, 2)]
+                block(psi_send, slot, per), block(final.at[mine_at], index, per), recv_sem.at[FINAL + index]
             ).start()
 
         def fill_cross(k, s, x):
@@ -496,7 +501,7 @@
                 if ahead is not None:
                     fill_cross(ahead, s, psi)
                 if s == 2:
-                    send_plain(psi)
+                    send_plain(psi, order[:3])
                 for rank in SEND[s][0]:
                     far_first(to_final, (rank,))
                 total = reduced(part.at[s], rs_buf.at[s], RS + s)
@@ -508,11 +513,14 @@
             if s == SECTIONS - 1:
                 far_first(lambda j: remote(held, held, AG + s, peer(j)).start(), (0, 2))
             if s in CHAINED and s < SECTIONS - 1:
-                psi = swap(apply(psi, fitted), order[s], per)
+                plain = apply(psi, fitted)
+                psi = swap(plain, order[s], per)
+                if s == 2:
+                    send_plain(plain, order[:2])
+                for rank in SEND[s][0]:
+                    far_first(to_final, (rank,))
                 if ahead is not None:
                     fill_cross(ahead, s, psi)
-                if s == 2:
-                    send_plain(psi)
             for rank in BACK[s]:
                 far_first(adj_back, (rank,))
             for rank in SEND[s][1]:
@@ -543,7 +551,7 @@
         departed(block(adj_in, 0, (owners - 1) * per), ADJ_IN)
         departed(block(psi_in, 0, (owners - 1) * per), PSI_IN)
         departed(block(adj_send, 0, (n - 1) * per), ADJ_OUT)
-        departed(block(psi_send, 0, (n - 1) * per), FINAL + lax.div(index, 2))
+        departed(block(psi_send, 0, (n - 1) * per), FINAL + index)
         departed(half_gate.at[0], HALF)
 
     @pl.when(jnp.logical_not(is_owner))
@@ -558,7 +566,8 @@
         departed(adj_in, ADJ_IN)
         departed(psi_in, PSI_IN)
 
-    departed(final.at[mine_at], FAR)
+    for k in range(chunks):
+        departed(block(final.at[mine_at], 0, pair), FAR + k)
     departed(final.at[pl.ds(0, 2)], NEAR)
     arrived(adj_out, ADJ_OUT)
 

time: 66.4 us -> 63.9 us (0.962)
  Pallas kernels: 64.2 us -> 61.7 us
    pallas_call x1, Pallas kernels: 64.2 us -> 61.7 us  [shards(): pl.pallas_call(functools.partial(kernel, used, order, extra_bits), out_sh...]
where the time goes in v4:
time: 63.9 us; the launch traced here: 63.7 us
  Pallas kernels  61.7 us (97%)
  local copies, waits for them, and re-layouts  1.41 us (2%)
  between operations  0.64 us (1%)
    pallas_call x1, Pallas kernels, shards(): pl.pallas_call(functools.partial(kernel, used, order, extra_bits), out_sh...  61.7 us
    unnamed x2, local copies, waits for them, and re-layouts  1.41 us

profile of v4, /device:TPU:0, one launch (start us, length us, event | category | flops | bytes accessed | tf_op | source)
XLA Modules:
  0.0 63.7 jit_solution(17368488375644977646)
XLA Ops:
  0.6 61.7 %sweep.1 = (f32[2,256,128]{2,1,0:T(8,128)S(1)}, f32[2,256,128]{2,1,0:T(8,128)S(1)}) custom-call(f32[2,256,128]{2,1,0:T(8,128)} %psi_in.1, f32[2,256,128]{2,1,0:T(8,128)} %adj_in.1, f32[4,2,128,128]{3,2,1,0:T(8,128)} %gates_in.1), custom_call_target="tpu_custom_call" | custom-call | tf_op jit(solution)/shard_map/sweep/pallas_call | solution.py:590
  62.3 0.7 %copy.7 = f32[2,256,128]{2,1,0:T(8,128)} copy(f32[2,256,128]{2,1,0:T(8,128)S(1)} %get-tuple-element.2) | data formatting | bytes 524288
  63.0 0.7 %copy.8 = f32[2,256,128]{2,1,0:T(8,128)} copy(f32[2,256,128]{2,1,0:T(8,128)S(1)} %get-tuple-element.3) | data formatting | bytes 524288

commit v5 on v4

--- a/solution.py
+++ b/solution.py
@@ -10,12 +10,12 @@
 SECTIONS = 4
 NS_ITERS = 8
 MESH = pl.DeviceIdType.MESH
-ADJ_IN, PSI_IN, ADJ_OUT, NEAR, HALF, FAR, FINAL, RS, AG, CROSS = 0, 1, 2, 3, 4, 5, 9, 17, 21, 25
+ADJ_IN, PSI_IN, ADJ_OUT, NEAR, HALF, FAR, FINAL, RS, AG, EXTRA, MIRROR, CROSS = 0, 1, 2, 3, 4, 5, 9, 17, 21, 25, 26, 27
 CHAINED = (1, 2, 3)
 CORE = CROSS + len(CHAINED)
 PHASES = CORE + 2 * len(CHAINED)
-BACK = ((0, 1), (), (), (), (2, 3))
-SEND = (((), ()), ((), ()), ((2, 3), (0, 1)), ((), ()))
+BACK = ((), (0,), (1,), (), (2, 3))
+SEND = (((), ()), ((), ()), ((2, 3), ()), ((), ()))
 
 
 def split(x):
@@ -136,7 +136,7 @@
     used, order, extra_bits,
     psi_in, adj_in, gates_in, psi_out, adj_out,
     psi_buf, adj_buf, gates, phi_t, phi_cross, psi_send, adj_send,
-    part, rs_buf, cross, pair_buf, chip_buf, cross_buf, ag_buf, final, half_gate, mid_buf, mid_cross,
+    psi_twin, twin_send, part, rs_buf, cross, pair_buf, chip_buf, cross_buf, ag_buf, final, half_gate, mid_buf, mid_cross,
     send_sem, recv_sem, mid_send, mid_recv, local_sem,
 ):
     group = lax.axis_index("groups")
@@ -282,34 +282,55 @@
     def target_variant(j):
         return variant(lax.rem(lax.div(j, 2 ** order[2]), 2), lax.rem(lax.div(j, 2 ** order[3]), 2))
 
-    def to_final(j):
-        remote(
-            block(psi_send, j, per),
-            block(final.at[target_variant(j)], index, per),
-            FINAL + index,
-            peer(j),
-        ).start()
+    def to_final(src, at, j):
+        there = j + (far_bit - lax.rem(lax.div(j, 2 ** order[3]), 2)) * 2 ** order[3]
+        remote(src(j), block(final.at[target_variant(j)], at, per), FINAL + at, peer(there)).start()
+
+    def to_final_chip(src, at):
+        for far in range(2):
+            j = slot + (far - far_bit) * 2 ** order[3]
+            pltpu.make_async_copy(
+                src(j),
+                block(final.at[variant(near_bit, far)], at, per),
+                recv_sem.at[FINAL + at],
+            ).start()
+            to_final(src, at, j + (1 - 2 * near_bit) * 2 ** order[2])
+
+    def to_final_side(src, at):
+        far_first(lambda j: to_final(src, at, j), (2,))
+        to_final_chip(src, at)
+
+    def over_slices(fn, side_far):
+        def step(k, carry):
+            half = lax.rem(lax.div(k, 2) + upper, 2)
+            fn(2 * half + lax.rem(k, 2), 4 * half + 2 * side_far + lax.rem(k, 2))
+            return carry
+
+        lax.fori_loop(0, chunks, step, 0)
+
+    def slices(k):
+        return [block(final.at[variant(near_bit, far)], k, per) for far in range(2)]
+
+    def two_blocks():
+        return block(final.at[mine_at], 0, pair)
 
     def pass_across():
-        def step(k, carry):
-            part_k = lax.rem(k + upper * (owners // 2), owners)
-            ref = block(final.at[mine_at], part_k, per)
-            arrived(ref, FINAL + part_k)
-            remote(ref, ref, FAR + lax.div(part_k, 2), flipped(order[3])).start()
-            remote(ref, ref, NEAR, flipped(order[2])).start()
-            return carry
-
-        lax.fori_loop(0, owners, step, 0)
+        def step(chunk, k):
+            arrived(two_blocks(), FINAL + k)
+            for ref in slices(k):
+                remote(ref, ref, FAR + chunk, flipped(order[3])).start()
+            for ref in slices(k):
+                remote(ref, ref, NEAR, flipped(order[2])).start()
+
+        over_slices(step, far_bit)
 
     def gather_final():
-        def step(k, carry):
-            part_k = lax.rem(k + upper * (chunks // 2), chunks)
-            ref = block(final.at[other_at], part_k, pair)
-            arrived(ref, FAR + part_k)
-            remote(ref, ref, NEAR, flipped(order[2])).start()
-            return carry
-
-        lax.fori_loop(0, chunks, step, 0)
+        def step(chunk, k):
+            arrived(two_blocks(), FAR + chunk)
+            for ref in slices(k):
+                remote(ref, ref, NEAR, flipped(order[2])).start()
+
+        over_slices(step, 1 - far_bit)
         arrived(final.at[pl.ds(0, 2)], NEAR)
 
     def keep_half(k, bit, x):
@@ -341,6 +362,29 @@
 
     owners_far_first(inward(adj_in, adj_buf, ADJ_IN))
     owners_far_first(inward(psi_in, psi_buf, PSI_IN))
+
+    def twin(k):
+        return lax.rem(k + owners // 2, owners)
+
+    side = first + upper * (owners // 2)
+    half_held = n * per // 2
+
+    def near_owners(fn):
+        for k in range(1, owners // 2 + 1):
+            j = side + lax.rem(slot + k, owners // 2)
+            if k < owners // 2:
+                fn(j)
+            else:
+
+                @pl.when(jnp.logical_not(is_owner))
+                def _():
+                    fn(j)
+
+    near_owners(
+        lambda j: remote(
+            block(psi_in, twin(j - first), per), block(psi_twin, slot, per), EXTRA, peer(j)
+        ).start()
+    )
 
     def put(ref, x, done):
         for q in done[::-1]:
@@ -375,6 +419,7 @@
         gate_copy.start()
         own_copy(block(adj_in, index, per), block(adj_buf, slot, per), ADJ_IN).start()
         own_copy(block(psi_in, index, per), block(psi_buf, slot, per), PSI_IN).start()
+        own_copy(block(psi_in, twin(index), per), block(psi_twin, slot, per), EXTRA).start()
         chip = lax.div(index, 2)
         parity = lax.rem(index, 2)
         mine = pl.ds(pl.multiple_of(shard(index) * own, own), own)
@@ -457,11 +502,23 @@
                 total = total + cross_buf[k, j]
             return total
 
+        def twin_first(u):
+            arrived(block(psi_twin, 0, half_held), EXTRA)
+            arrived(block(psi_twin, 0, half_held), MIRROR)
+            x = swap(apply(swap(joined(psi_twin), order[0], per), u), order[0], per)
+            return jnp.where(upper == 0, x[:half_held], x[half_held:])
+
+        def send_twin(x, u):
+            x = swap(apply(swap(x, order[1], per), u), order[1], per)
+            twin_send[0] = x[:, :gate]
+            twin_send[1] = x[:, gate:]
+            at = twin(index)
+
+            to_final_side(lambda j: block(twin_send, j - upper * (n // 2), per), at)
+
         def send_plain(x, done):
             put(psi_send, x, done)
-            pltpu.make_async_copy(
-                block(psi_send, slot, per), block(final.at[mine_at], index, per), recv_sem.at[FINAL + index]
-            ).start()
+            to_final_side(lambda j: block(psi_send, j, per), index)
 
         def fill_cross(k, s, x):
             state = split(x)
@@ -502,8 +559,6 @@
                     fill_cross(ahead, s, psi)
                 if s == 2:
                     send_plain(psi, order[:3])
-                for rank in SEND[s][0]:
-                    far_first(to_final, (rank,))
                 total = reduced(part.at[s], rs_buf.at[s], RS + s)
                 if extra > 1:
                     total = over_layers(mid_buf.at[s], total, s)
@@ -517,17 +572,20 @@
                 psi = swap(plain, order[s], per)
                 if s == 2:
                     send_plain(plain, order[:2])
-                for rank in SEND[s][0]:
-                    far_first(to_final, (rank,))
                 if ahead is not None:
                     fill_cross(ahead, s, psi)
+                if s == 2:
+                    send_twin(twin_state, fitted)
             for rank in BACK[s]:
                 far_first(adj_back, (rank,))
-            for rank in SEND[s][1]:
-                far_first(to_final, (rank,))
             if s == SECTIONS - 1:
                 pass_across()
             arrived(block(ag_buf.at[s], 0, (owners - 1) * own), AG + s)
+            if s == 0:
+                theirs = block(psi_buf, upper, half_held)
+                remote(theirs, block(psi_twin, upper, half_held), MIRROR, peer(first + twin(index))).start()
+            if s == 1:
+                twin_state = twin_first(fitted)
             fitted = fit(s)
             if s == SECTIONS - 2:
                 share_half(0, near_bit, fitted)
@@ -551,7 +609,10 @@
         departed(block(adj_in, 0, (owners - 1) * per), ADJ_IN)
         departed(block(psi_in, 0, (owners - 1) * per), PSI_IN)
         departed(block(adj_send, 0, (n - 1) * per), ADJ_OUT)
-        departed(block(psi_send, 0, (n - 1) * per), FINAL + index)
+        departed(block(psi_send, 0, (n // 2 - 2) * per), FINAL + index)
+        departed(block(psi_send, 0, (n // 2 - 2) * per), FINAL + twin(index))
+        departed(block(psi_in, 0, (owners // 2 - 1) * per), EXTRA)
+        departed(block(psi_twin, 0, half_held), MIRROR)
         departed(half_gate.at[0], HALF)
 
     @pl.when(jnp.logical_not(is_owner))
@@ -565,6 +626,7 @@
         last(x)
         departed(adj_in, ADJ_IN)
         departed(psi_in, PSI_IN)
+        departed(block(psi_in, 0, owners // 2 * per), EXTRA)
 
     for k in range(chunks):
         departed(block(final.at[mine_at], 0, pair), FAR + k)
@@ -600,6 +662,8 @@
                 pltpu.VMEM((len(CHAINED), 2, 2, 2 * gate, held // 2), bf16),
                 pltpu.VMEM((2, held, gate), f32),
                 pltpu.VMEM((2, held, gate), f32),
+                pltpu.VMEM((2, held, gate), f32),
+                pltpu.VMEM((2, held // 2, gate), f32),
                 pltpu.VMEM((SECTIONS, 2, gate, gate), f32),
                 pltpu.VMEM((SECTIONS, owners, 2, own, gate), f32),
                 pltpu.VMEM((len(CHAINED), 8, gate, gate), f32),

time: 63.9 us -> 62.6 us (0.980)
  Pallas kernels: 61.7 us -> 59.8 us
    pallas_call x1, Pallas kernels: 61.7 us -> 59.8 us  [shards(): pl.pallas_call(functools.partial(kernel, used, order, extra_bits), out_sh...]
where the time goes in v5:
time: 62.6 us; the launch traced here: 61.9 us
  Pallas kernels  59.8 us (96%)
  local copies, waits for them, and re-layouts  1.41 us (2%)
  between operations  0.64 us (1%)
    pallas_call x1, Pallas kernels, shards(): pl.pallas_call(functools.partial(kernel, used, order, extra_bits), out_sh...  59.8 us
    unnamed x2, local copies, waits for them, and re-layouts  1.41 us

profile of v5, /device:TPU:0, one launch (start us, length us, event | category | flops | bytes accessed | tf_op | source)
XLA Modules:
  0.0 61.9 jit_solution(10876368231497809215)
XLA Ops:
  0.6 59.8 %sweep.1 = (f32[2,256,128]{2,1,0:T(8,128)S(1)}, f32[2,256,128]{2,1,0:T(8,128)S(1)}) custom-call(f32[2,256,128]{2,1,0:T(8,128)} %psi_in.1, f32[2,256,128]{2,1,0:T(8,128)} %adj_in.1, f32[4,2,128,128]{3,2,1,0:T(8,128)} %gates_in.1), custom_call_target="tpu_custom_call" | custom-call | tf_op jit(solution)/shard_map/sweep/pallas_call | solution.py:652
  60.5 0.7 %copy.7 = f32[2,256,128]{2,1,0:T(8,128)} copy(f32[2,256,128]{2,1,0:T(8,128)S(1)} %get-tuple-element.2) | data formatting | bytes 524288
  61.2 0.7 %copy.8 = f32[2,256,128]{2,1,0:T(8,128)} copy(f32[2,256,128]{2,1,0:T(8,128)S(1)} %get-tuple-element.3) | data formatting | bytes 524288

commit v6 on v5

--- a/solution.py
+++ b/solution.py
@@ -566,7 +566,7 @@
             held = block(ag_buf.at[s], shard(index), own)
             among(lambda j: remote(held, held, AG + s, peer(j)).start())
             if s == SECTIONS - 1:
-                far_first(lambda j: remote(held, held, AG + s, peer(j)).start(), (0, 2))
+                far_first(lambda j: remote(held, held, AG + s, peer(j)).start(), (2, 0))
             if s in CHAINED and s < SECTIONS - 1:
                 plain = apply(psi, fitted)
                 psi = swap(plain, order[s], per)

time: 62.6 us -> 62.6 us (level)
  no operation moved by 1% of the time
where the time goes in v6:
time: 62.6 us; the launch traced here: 61.9 us
  Pallas kernels  59.8 us (96%)
  local copies, waits for them, and re-layouts  1.41 us (2%)
  between operations  0.64 us (1%)
    pallas_call x1, Pallas kernels, shards(): pl.pallas_call(functools.partial(kernel, used, order, extra_bits), out_sh...  59.8 us
    unnamed x2, local copies, waits for them, and re-layouts  1.41 us

profile of v6, /device:TPU:0, one launch (start us, length us, event | category | flops | bytes accessed | tf_op | source)
XLA Modules:
  0.0 61.9 jit_solution(1132028577458674298)
XLA Ops:
  0.6 59.8 %sweep.1 = (f32[2,256,128]{2,1,0:T(8,128)S(1)}, f32[2,256,128]{2,1,0:T(8,128)S(1)}) custom-call(f32[2,256,128]{2,1,0:T(8,128)} %psi_in.1, f32[2,256,128]{2,1,0:T(8,128)} %adj_in.1, f32[4,2,128,128]{3,2,1,0:T(8,128)} %gates_in.1), custom_call_target="tpu_custom_call" | custom-call | tf_op jit(solution)/shard_map/sweep/pallas_call | solution.py:652
  60.5 0.7 %copy.7 = f32[2,256,128]{2,1,0:T(8,128)} copy(f32[2,256,128]{2,1,0:T(8,128)S(1)} %get-tuple-element.2) | data formatting | bytes 524288
  61.2 0.7 %copy.8 = f32[2,256,128]{2,1,0:T(8,128)} copy(f32[2,256,128]{2,1,0:T(8,128)S(1)} %get-tuple-element.3) | data formatting | bytes 524288
